TPU v7x, 32 devices: a whole 2x2x4 slice. The times are simulated.
32 devices in a mesh: grp: 4 (over z), dev: 8 (over y, x, core).
Axes of the slice: x: 2, y: 2, z: 4, core: 2. Of those that a mesh axis runs over, the one named last changes fastest.
Arguments:
- panel: float32 [32768, 512], P(('grp', 'dev')), may hold values from -45 to 45
- signs: int32 [32768], P(('grp', 'dev')), may hold values from 0 to 1
- source_group: int32 [4, 8, 32, 1], P(None, 'dev'), may hold values from 0 to 3; in each aligned block of 32 rows (0 to 31, 32 to 63, ..., all dimensions but the last counted through in order) at most 16 rows name the same one
- source_row: int32 [4, 8, 32], P(None, 'dev'), may hold values from 0 to 1023, as said below
Outputs:
- sketch: float32 [1024, 512], P(('grp', 'dev'))
- conditioned: float32 [32768, 512], P(('grp', 'dev'))
Inputs may be any that keep to these rules, and one draw needn't show every extreme that they name: Among the 32 entries source_group[g, d, :, 0] for one g and d, no group is named more than 16 times, and in some such block one group is named exactly 16 times. source_row[g, d, j] lies in the row band of owner j // 4: source_row[g, d, j] // 128 equals j // 4; the row within the band is free.
All inputs are finite; a program needn't handle non-finite values.
Results may differ from a plain program's by a relative error of at most 0.00013.
Values sent between devices are 32-bit elements; how exact they have to be, the bound alone decides.
A program may use at most 64 MiB of HBM per device.

v0:
```python
import functools
import math
import jax
import jax.numpy as jnp
from jax import lax
from jax.experimental import pallas as pl
from jax.experimental.pallas import tpu as pltpu
from jax.sharding import PartitionSpec as P

BLOCK = 128


def pivot_block(tiles):
    count = len(tiles)
    lane = lax.broadcasted_iota(jnp.int32, (8, BLOCK), 1)
    sub = lax.broadcasted_iota(jnp.int32, (8, BLOCK), 0)
    tiles = list(tiles)
    for p in range(count):
        base = 8 * p
        inside = (lane >= base) & (lane < base + 8)
        cols = {
            q: [jnp.broadcast_to(tiles[q][:, base + t : base + t + 1], (8, BLOCK)) for t in range(8)]
            for q in range(p, count)
        }
        tiles[p] = jnp.where(inside, (lane - base == sub).astype(jnp.float32), tiles[p])
        for q in range(p + 1, count):
            tiles[q] = jnp.where(inside, 0.0, tiles[q])
        diag = jnp.ones((8, BLOCK), jnp.float32)
        for t in range(8):
            pivot = jnp.broadcast_to(cols[p][t][t : t + 1, :], (8, BLOCK))
            diag = jnp.where(sub == t, pivot, diag)
            inverse = 1.0 / pivot
            row = jnp.broadcast_to(tiles[p][t : t + 1, :], (8, BLOCK)) * inverse
            heads = [
                jnp.broadcast_to(cols[p][u][t : t + 1, :], (8, BLOCK)) * inverse for u in range(t + 1, 8)
            ]
            for q in range(p, count):
                coef = cols[q][t]
                if q == p:
                    coef = jnp.where(sub > t, coef, 0.0)
                for place, u in enumerate(range(t + 1, 8)):
                    cols[q][u] = cols[q][u] - coef * heads[place]
                tiles[q] = tiles[q] - coef * row
        tiles[p] = tiles[p] * lax.rsqrt(diag)
    return tiles


def matmul(a, b, dims):
    return lax.dot_general(
        a, b, (dims, ((), ())), precision=lax.Precision.HIGHEST, preferred_element_type=jnp.float32
    )


def inverse_factor(work):
    size = work.shape[0]
    rowi = lax.broadcasted_iota(jnp.int32, (BLOCK, BLOCK), 0)
    coli = lax.broadcasted_iota(jnp.int32, (BLOCK, BLOCK), 1)
    wide = lax.broadcasted_iota(jnp.int32, (BLOCK, size), 1)

    def step(k, carry):
        start = pl.multiple_of(k * BLOCK, BLOCK)
        here = pl.ds(start, BLOCK)
        tiles = [
            work[pl.ds(pl.multiple_of(start + 8 * p, 8), 8), here] for p in range(BLOCK // 8)
        ]
        tiles = pivot_block(tiles)
        own = jnp.where(rowi >= coli, jnp.concatenate(tiles, axis=0), 0.0)
        rows = matmul(own, work[here, :], ((1,), (0,)))
        work[here, :] = rows
        work[here, here] = own
        rows = work[here, :]
        work[:, here] = jnp.where(
            lax.broadcasted_iota(jnp.int32, (size, BLOCK), 0) >= start + BLOCK, 0.0, work[:, here]
        )
        left = jnp.where(wide >= start + BLOCK, rows, 0.0)
        work[...] = work[...] - matmul(left, rows, ((0,), (0,)))
        work[here, :] = jnp.where(wide < start + BLOCK, rows, 0.0)
        return carry

    lax.fori_loop(0, size // BLOCK, step, 0)


def add_ridge(gram, sketch_total):
    size = gram.shape[0]
    rowi = lax.broadcasted_iota(jnp.int32, (size, size), 0)
    coli = lax.broadcasted_iota(jnp.int32, (size, size), 1)
    return gram / sketch_total + jnp.where(rowi == coli, 0.001, 0.0)


def gram_kernel(sketch_total, sketch_ref, out_ref, work):
    sketch = sketch_ref[...]
    work[...] = add_ridge(matmul(sketch, sketch, ((0,), (0,))), sketch_total)
    inverse_factor(work)
    out_ref[...] = work[...]


def from_gram_kernel(sketch_total, gram_ref, out_ref, work):
    work[...] = add_ridge(gram_ref[...], sketch_total)
    inverse_factor(work)
    out_ref[...] = work[...]


def bit_parity(value, bits):
    total = jnp.zeros_like(value)
    for bit_place in range(bits):
        total = total + (value >> bit_place & 1)
    return total & 1


def sylvester(order):
    index = jnp.arange(order, dtype=jnp.int32)
    parity = bit_parity(index[:, None] & index[None, :], order.bit_length())
    return (1 - 2 * parity).astype(jnp.float32)


def on_device(panel, signs, source_group, source_row):
    rows_here = panel.shape[0]
    columns = panel.shape[1]
    groups = lax.axis_size("grp")
    devices = lax.axis_size("dev")
    group_here = lax.axis_index("grp")
    highest = lax.Precision.HIGHEST
    flipped = panel * (1 - 2 * signs).astype(jnp.float32)[:, None]
    local = jnp.dot(
        sylvester(rows_here), flipped, precision=highest, preferred_element_type=jnp.float32
    )
    dev_table = sylvester(devices)
    mixed = jnp.einsum(
        "ed,dbc->ebc",
        dev_table,
        lax.all_to_all(
            local.reshape(devices, rows_here // devices, columns),
            "dev",
            split_axis=0,
            concat_axis=0,
            tiled=True,
        ),
        precision=highest,
    )
    inner = mixed
    inner = inner.reshape(rows_here, columns)
    chosen_group = source_group[:, 0, :, 0]
    chosen_row = source_row[:, 0, :]
    width = chosen_group.shape[1]
    per_owner = width // devices
    band_size = rows_here // devices
    dev_here = lax.axis_index("dev")
    stacked = jnp.stack([chosen_group, chosen_row]).reshape(2, groups, devices, per_owner)
    lists = lax.all_to_all(stacked, "dev", split_axis=2, concat_axis=2, tiled=True)
    band_group = lists[0].reshape(-1)
    band_row = lists[1].reshape(-1)
    flat_place = jnp.arange(groups * devices * per_owner, dtype=jnp.int32)
    source_dev = flat_place // per_owner % devices
    flat_index = source_dev * band_size + band_row - dev_here * band_size
    parity = bit_parity(band_group & group_here, groups.bit_length())
    factor = (1 - 2 * parity).astype(jnp.float32)
    gathered = lax.psum_scatter(
        inner[flat_index] * factor[:, None], "grp", scatter_dimension=0, tiled=True
    )
    panel_total = rows_here * devices * groups
    sketch = gathered * (1.0 / math.sqrt(panel_total))
    sketch_total = sketch.shape[0] * devices * groups
    if sketch_total <= rows_here:
        pieces = lax.all_gather(sketch, ("grp", "dev"), axis=0, tiled=True)
        kernel = functools.partial(gram_kernel, sketch_total)
    else:
        partial_gram = jnp.dot(sketch.T, sketch, precision=highest, preferred_element_type=jnp.float32)
        pieces = lax.psum(partial_gram, ("grp", "dev"))
        kernel = functools.partial(from_gram_kernel, sketch_total)
    inverse = pl.pallas_call(
        kernel,
        out_shape=jax.ShapeDtypeStruct((columns, columns), jnp.float32),
        in_specs=[pl.BlockSpec(memory_space=pltpu.VMEM)],
        out_specs=pl.BlockSpec(memory_space=pltpu.VMEM),
        scratch_shapes=[pltpu.VMEM((columns, columns), jnp.float32)],
        name="factor",
    )(pieces)
    conditioned = lax.dot_general(
        panel, inverse, (((1,), (1,)), ((), ())), precision=highest, preferred_element_type=jnp.float32
    )
    return (sketch, conditioned)


def solution(mesh):
    return jax.shard_map(
        on_device,
        mesh=mesh,
        in_specs=(
            P(("grp", "dev"), None),
            P(("grp", "dev")),
            P(None, "dev", None, None),
            P(None, "dev", None),
        ),
        out_specs=(P(("grp", "dev"), None), P(("grp", "dev"), None)),
        check_vma=False,
    )
```

profile of v0, /device:TPU:0, one launch (start us, length us, event | category | flops | bytes accessed | tf_op | source)
XLA Modules:
  0.0 187.8 jit_solution(8617679664391923073)
XLA Ops:
  7.2 0.5 broadcast.219
  7.7 1.3 reduce.7
  9.0 1.3 reduce.6
  10.4 0.1 stack.8
  10.4 0.1 stack.7
  10.5 0.6 copy.19
  11.2 5.2 %all-to-all-start.1 = ((s32[2,4,8,4]{3,1,0,2:T(4,128)}), s32[2,4,8,4]{3,1,0,2:T(4,128)S(1)}, u32[]{:S(2)}, u32[]{:S(2)}) async-start(s32[2,4,8,4]{3,1,0,2:T(4,128)} %copy.19), calls=%async_computation.1 | async-start | bytes 65536 | tf_op jit(solution)/shard_map/all_to_all | solution.py:149
  16.4 0.7 subtract_convert_fusion.1
  17.1 14.7 %fusion = f32[1024,512]{1,0:T(8,128)} fusion(f32[1024,512]{1,0:T(8,128)} %param.4, f32[1024]{0:T(1024)S(1)} %subtract_convert_fusion.1), kind=kOutput, calls=%fused_computation.1 | convolution fusion | flops 6481772544 | bytes 4198400 | tf_op jit(solution)/shard_map/dot_general | solution.py:124
  31.8 0.0 all-to-all-done.1
  31.8 4.2 %all-to-all-start = ((f32[8,128,512]{2,1,0:T(8,128)}), f32[8,128,512]{2,1,0:T(8,128)S(1)}, u32[]{:S(2)}, u32[]{:S(2)}) async-start(f32[8,128,512]{2,1,0:T(8,128)} %bitcast.17), calls=%async_computation | async-start | bytes 4194304 | tf_op jit(solution)/shard_map/all_to_all | solution.py:131
  36.0 0.2 reduce-scatter.2.cloned.1.call-start
  36.2 0.1 copy.24
  36.4 0.1 copy.22
  36.5 0.1 reshape.157
  36.6 0.1 reshape_squeeze.4
  36.7 25.9 %all-to-all-done = f32[8,128,512]{2,1,0:T(8,128)S(1)} async-done(((f32[8,128,512]{2,1,0:T(8,128)}), f32[8,128,512]{2,1,0:T(8,128)S(1)}, u32[]{:S(2)}, u32[]{:S(2)}) %all-to-all-start) | async-done | bytes 2097184 | tf_op jit(solution)/shard_map/all_to_all | solution.py:131
  62.6 2.9 %fusion.40 = f32[8,128,512]{2,0,1:T(8,128)S(1)} fusion(f32[8,128,512]{2,1,0:T(8,128)S(1)} %all-to-all-done), kind=kOutput, calls=%fused_computation.41 | convolution fusion | flops 50332672 | bytes 4194304 | tf_op jit(solution)/shard_map/ed,dbc->ebc/dot_general | solution.py:128
  65.5 1.2 copy.18
  66.7 0.8 gather_fusion
  67.5 0.8 broadcast_multiply_fusion
  68.3 0.0 reduce-scatter.2.cloned.1.call-update
  68.3 0.0 all-gather.2.cloned.1.call-start
  68.3 19.5 %reduce-scatter.2.cloned.1.call-done = f32[32,512]{1,0:T(8,128)} async-done(((f32[128,512]{1,0:T(8,128)}), f32[32,512]{1,0:T(8,128)}) %reduce-scatter.2.cloned.1.call-update) | async-done | bytes 65552 | tf_op jit(solution)/shard_map/reduce_scatter | solution.py:157
  87.8 1.5 broadcast_multiply_fusion.1
  89.3 0.0 all-gather.2.cloned.1.call-update
  89.3 56.4 %all-gather.2.cloned.1.call-done.sketch_ref = f32[1024,512]{1,0:T(8,128)} async-done(((f32[32,512]{1,0:T(8,128)}), f32[1024,512]{1,0:T(8,128)}) %all-gather.2.cloned.1.call-update) | async-done | bytes 2097168 | tf_op jit(solution)/shard_map/all_gather | solution.py:164
  145.7 27.9 %factor.1 = f32[512,512]{1,0:T(8,128)} custom-call(f32[1024,512]{1,0:T(8,128)} %all-gather.2.cloned.1.call-done.sketch_ref), custom_call_target="tpu_custom_call" | custom-call | tf_op jit(solution)/shard_map/factor/pallas_call | solution.py:170
  173.7 5.5 %convolution_bitcast_fusion = f32[1024,512]{0,1:T(8,128)S(1)} fusion(f32[512,512]{1,0:T(8,128)} %factor.1, f32[1024,512]{1,0:T(8,128)} %param.4), kind=kOutput, calls=%fused_computation.55 | convolution fusion | flops 3221225472 | bytes 5242880 | tf_op jit(solution)/shard_map/dot_general | solution.py:178
  179.2 1.8 copy.23
  (6 shorter events, 0.1 us)
Async XLA Ops:
  11.2 20.6 %all-to-all-start.1 = ((s32[2,4,8,4]{3,1,0,2:T(4,128)}), s32[2,4,8,4]{3,1,0,2:T(4,128)S(1)}, u32[]{:S(2)}, u32[]{:S(2)}) async-start(s32[2,4,8,4]{3,1,0,2:T(4,128)} %copy.19), calls=%async_computation.1 | async-start | bytes 65536 | tf_op jit(solution)/shard_map/all_to_all | solution.py:149
  31.8 30.8 %all-to-all-start = ((f32[8,128,512]{2,1,0:T(8,128)}), f32[8,128,512]{2,1,0:T(8,128)S(1)}, u32[]{:S(2)}, u32[]{:S(2)}) async-start(f32[8,128,512]{2,1,0:T(8,128)} %bitcast.17), calls=%async_computation | async-start | bytes 4194304 | tf_op jit(solution)/shard_map/all_to_all | solution.py:131
  36.0 51.8 %reduce-scatter.2.cloned.1.call-start = ((), (), s32[]{:S(2)}) async-start(), calls=%async_computation.3 | async-start | bytes 327680 | tf_op jit(solution)/shard_map/reduce_scatter | solution.py:157
  68.3 77.5 %all-gather.2.cloned.1.call-start = ((), (), s32[]{:S(2)}) async-start(), calls=%async_computation.4 | async-start | bytes 2162688 | tf_op jit(solution)/shard_map/all_gather | solution.py:164
Sparse Core Ops, SparseCore 0:
  68.4 19.3 reduce-scatter.1
  91.3 54.4 all-gather.1
where the time goes:
time: 188 us
  waiting for transfers between devices  102 us (54%)
  Pallas kernels  27.9 us (15%)
  matrix products  23.1 us (12%)
  between operations  14.1 us (8%)
  starting transfers between devices  9.66 us (5%)
  other arithmetic  5.7 us (3%)
  local copies, waits for them, and re-layouts  5.51 us (3%)
    all_gather x1, waiting for transfers between devices, on_device(): pieces = lax.all_gather(sketch, ('grp', 'dev'), axis=0, tiled=True)  56.4 us
    pallas_call x1, Pallas kernels, on_device(): pl.pallas_call(kernel, out_shape=jax.ShapeDtypeStruct((columns, columns),...  27.9 us
    all_to_all x1, waiting for transfers between devices, on_device(): lax.all_to_all(local.reshape(devices, rows_here // devices, columns), 'de...  25.9 us
    reduce_scatter x1, waiting for transfers between devices, on_device(): lax.psum_scatter(inner[flat_index] * factor[:, None], 'grp', scatter_dime...  19.5 us
    dot_general x1, matrix products, on_device(): jnp.dot(sylvester(rows_here), flipped, precision=highest, preferred_eleme...  14.7 us
    dot_general x1, matrix products, on_device(): lax.dot_general(panel, inverse, (((1,), (1,)), ((), ())), precision=highe...  5.48 us
    all_to_all x1, starting transfers between devices, on_device(): lax.all_to_all(stacked, 'dev', split_axis=2, concat_axis=2, tiled=True)  5.2 us
    all_to_all x1, starting transfers between devices, on_device(): lax.all_to_all(local.reshape(devices, rows_here // devices, columns), 'de...  4.2 us
  transfers between devices with their start and end apart: 4, of which 3 were waited for; matrix products, arithmetic and copies ran while one was open for 8% of the time, Pallas kernels for 0%

commit v1 on v0

--- a/solution.py
+++ b/solution.py
@@ -100,6 +100,230 @@
     out_ref[...] = work[...]
 
 
+def flip(index, mask):
+    bit = 1
+    while bit <= mask:
+        if mask & bit:
+            index = index + bit - 2 * bit * lax.rem(lax.div(index, bit), 2)
+        bit = 2 * bit
+    return index
+
+
+def parity_sign(value, bits):
+    span = 1
+    while span < bits:
+        span = span * 2
+    while span > 1:
+        span = span // 2
+        value = value ^ (value >> span)
+    return (1 - 2 * (value & 1)).astype(jnp.float32)
+
+
+def sketch_kernel(
+    groups, per_owner, scale, panel_ref, signs_ref, picks_ref, whole_ref, own_ref,
+    lists, high, low, choice, acc, from_core, from_first, from_second, from_group, send, recv,
+):
+    devices = 8
+    rows_here, columns = panel_ref.shape
+    half = columns // 2
+    left, right = pl.ds(0, half), pl.ds(half, half)
+    band = groups * devices * per_owner
+    share = devices * per_owner
+    me = lax.axis_index("dev")
+    here = lax.axis_index("grp")
+
+    barrier = pltpu.get_barrier_semaphore()
+    for mask in range(1, devices):
+        pl.semaphore_signal(
+            barrier, inc=1, device_id={"dev": flip(me, mask)}, device_id_type=pl.DeviceIdType.MESH
+        )
+    for mask in range(1, groups):
+        pl.semaphore_signal(
+            barrier, inc=1, device_id={"grp": flip(here, mask)}, device_id_type=pl.DeviceIdType.MESH
+        )
+    pl.semaphore_wait(barrier, devices + groups - 2)
+
+    taken = []
+
+    def transfer(source, target, axis, mask):
+        place = len(taken)
+        taken.append(place)
+        peer = flip(me if axis == "dev" else here, mask)
+        copy = pltpu.make_async_remote_copy(
+            src_ref=source,
+            dst_ref=target,
+            send_sem=send.at[place],
+            recv_sem=recv.at[place],
+            device_id={axis: peer},
+            device_id_type=pl.DeviceIdType.MESH,
+        )
+        copy.start()
+        return copy
+
+    sends = []
+    listed = [transfer(picks_ref, lists.at[mask], "dev", mask) for mask in range(1, devices)]
+    flipped = panel_ref[...] * (1 - 2 * signs_ref[...]).astype(jnp.float32)
+    top = flipped.astype(jnp.bfloat16)
+    high[...] = top
+    low[...] = (flipped - top.astype(jnp.float32)).astype(jnp.bfloat16)
+    lists[0] = picks_ref[...]
+    for copy in listed:
+        copy.wait_recv()
+    sends += listed
+
+    slot = lax.broadcasted_iota(jnp.int32, (devices, band), 0)
+    group_of = jnp.concatenate([lists[m][0:1, :] for m in range(devices)], axis=0)
+    row_of = jnp.concatenate([lists[m][1:2, :] for m in range(devices)], axis=0)
+    value = (group_of * devices + (slot ^ me)) * rows_here + row_of
+    total = devices * band
+    place = lax.broadcasted_iota(jnp.int32, (total, band), 0)
+    entry = lax.broadcasted_iota(jnp.int32, (total, band), 1)
+    owner = (place // band) ^ me
+    group = ((place // share) % groups) ^ here
+    wanted = group * share + owner * per_owner + place % per_owner
+    spread = lax.dot_general(
+        (entry == wanted).astype(jnp.float32),
+        value.astype(jnp.float32),
+        (((1,), (1,)), ((), ())),
+        precision=lax.Precision.HIGHEST,
+        preferred_element_type=jnp.float32,
+    )
+    place = lax.broadcasted_iota(jnp.int32, (total, devices), 0)
+    held = lax.broadcasted_iota(jnp.int32, (total, devices), 1)
+    source = ((place // per_owner) % devices) ^ me
+    choice[...] = jnp.sum(jnp.where(held == source, spread, 0.0), axis=1, keepdims=True).astype(jnp.int32)
+
+    def mixed(chunk):
+        pick = jnp.broadcast_to(choice[chunk * band : (chunk + 1) * band, :], (band, 128))
+        lane = lax.broadcasted_iota(jnp.int32, (band, 128), 1)
+        rank = here * devices + me
+        above = parity_sign((pick // rows_here) & rank, (groups * devices).bit_length() - 1)
+        table = [parity_sign(pick & lane, 7) * above]
+        bit = 7
+        while 128 * len(table) < rows_here:
+            turn = (1 - 2 * ((pick >> bit) & 1)).astype(jnp.float32)
+            table = table + [part * turn for part in table]
+            bit = bit + 1
+        table = jnp.concatenate([part.astype(jnp.bfloat16) for part in table], axis=1)
+        dims = (((1,), (0,)), ((), ()))
+        return lax.dot_general(
+            table, high[...], dims, preferred_element_type=jnp.float32
+        ) + lax.dot_general(table, low[...], dims, preferred_element_type=jnp.float32)
+
+    core = {}
+    for chunk in (7, 3, 5, 1):
+        acc[chunk] = mixed(chunk)
+        core[chunk - 1] = transfer(acc.at[chunk], from_core.at[chunk // 2], "dev", 1)
+    first, second = {}, {}
+    for chunk in (6, 2, 4, 0):
+        acc[chunk] = mixed(chunk)
+        core[chunk].wait_recv()
+        acc[chunk] = acc[chunk] + from_core[chunk // 2]
+        if chunk & 2:
+            first["left", chunk - 2] = transfer(
+                acc.at[chunk, :, left], from_first.at[chunk // 4, :, left], "dev", 2
+            )
+        if chunk & 4:
+            first["right", chunk - 4] = transfer(
+                acc.at[chunk, :, right], from_first.at[(chunk & 2) // 2, :, right], "dev", 4
+            )
+    first["left", 4].wait_recv()
+    acc[4, :, left] = acc[4, :, left] + from_first[1, :, left]
+    second["left"] = transfer(acc.at[4, :, left], from_second.at[:, left], "dev", 4)
+    first["right", 2].wait_recv()
+    acc[2, :, right] = acc[2, :, right] + from_first[1, :, right]
+    second["right"] = transfer(acc.at[2, :, right], from_second.at[:, right], "dev", 2)
+    first["left", 0].wait_recv()
+    first["right", 0].wait_recv()
+    acc[0] = acc[0] + from_first[0]
+    second["left"].wait_recv()
+    second["right"].wait_recv()
+    acc[0] = acc[0] + from_second[...]
+    sends += list(core.values()) + list(first.values()) + list(second.values())
+    across = [
+        transfer(acc.at[0, pl.ds(block * share, share)], from_group.at[block], "grp", block)
+        for block in range(1, groups)
+    ]
+    result = acc[0, 0:share, :]
+    for block in range(1, groups):
+        across[block - 1].wait_recv()
+        result = result + from_group[block]
+    sends += across
+    result = result * scale
+    own_ref[...] = result
+    whole_ref[0, 0:share, :] = result
+
+    across = [
+        transfer(
+            whole_ref.at[0, pl.ds(0, share)], whole_ref.at[0, pl.ds(block * share, share)], "grp", block
+        )
+        for block in range(1, groups)
+    ]
+    for copy in across:
+        copy.wait_recv()
+    sends += across
+    out = [
+        transfer(whole_ref.at[0, :, left], whole_ref.at[4, :, left], "dev", 4),
+        transfer(whole_ref.at[0, :, right], whole_ref.at[2, :, right], "dev", 2),
+        transfer(whole_ref.at[0, :, left], whole_ref.at[2, :, left], "dev", 2),
+        transfer(whole_ref.at[0, :, right], whole_ref.at[4, :, right], "dev", 4),
+    ]
+    last = [transfer(whole_ref.at[0], whole_ref.at[1], "dev", 1)]
+    out[0].wait_recv()
+    relay = [transfer(whole_ref.at[4, :, left], whole_ref.at[6, :, left], "dev", 2)]
+    out[1].wait_recv()
+    relay.append(transfer(whole_ref.at[2, :, right], whole_ref.at[6, :, right], "dev", 4))
+    out[2].wait_recv()
+    last.append(transfer(whole_ref.at[2], whole_ref.at[3], "dev", 1))
+    out[3].wait_recv()
+    last.append(transfer(whole_ref.at[4], whole_ref.at[5], "dev", 1))
+    relay[0].wait_recv()
+    relay[1].wait_recv()
+    last.append(transfer(whole_ref.at[6], whole_ref.at[7], "dev", 1))
+    for copy in last:
+        copy.wait_recv()
+    sends += out + relay + last
+    for copy in sends:
+        copy.wait_send()
+
+
+def kernel_sketch(panel, signs, source_group, source_row, groups, devices):
+    rows_here, columns = panel.shape
+    per_owner = source_row.shape[2] // devices
+    band = groups * devices * per_owner
+    share = devices * per_owner
+    picks = jnp.stack([source_group.reshape(band), source_row.reshape(band)])
+    picks = jnp.concatenate([picks, jnp.zeros((6, band), jnp.int32)], axis=0)
+    scale = 1.0 / math.sqrt(rows_here * devices * groups)
+    vmem = pl.BlockSpec(memory_space=pltpu.VMEM)
+    f32 = jnp.float32
+    whole, own = pl.pallas_call(
+        functools.partial(sketch_kernel, groups, per_owner, scale),
+        out_shape=(
+            jax.ShapeDtypeStruct((devices, band, columns), f32),
+            jax.ShapeDtypeStruct((share, columns), f32),
+        ),
+        in_specs=[vmem] * 3,
+        out_specs=(vmem, vmem),
+        scratch_shapes=[
+            pltpu.VMEM((devices, 8, band), jnp.int32),
+            pltpu.VMEM((rows_here, columns), jnp.bfloat16),
+            pltpu.VMEM((rows_here, columns), jnp.bfloat16),
+            pltpu.VMEM((devices * band, 1), jnp.int32),
+            pltpu.VMEM((devices, band, columns), f32),
+            pltpu.VMEM((devices // 2, band, columns), f32),
+            pltpu.VMEM((2, band, columns), f32),
+            pltpu.VMEM((band, columns), f32),
+            pltpu.VMEM((groups, share, columns), f32),
+            pltpu.SemaphoreType.DMA((40,)),
+            pltpu.SemaphoreType.DMA((40,)),
+        ],
+        compiler_params=pltpu.CompilerParams(collective_id=0, has_side_effects=True),
+        name="sketch",
+    )(panel, signs[:, None], picks)
+    return whole.reshape(devices * band, columns), own
+
+
 def bit_parity(value, bits):
     total = jnp.zeros_like(value)
     for bit_place in range(bits):
@@ -113,7 +337,7 @@
     return (1 - 2 * parity).astype(jnp.float32)
 
 
-def on_device(panel, signs, source_group, source_row):
+def general_sketch(panel, signs, source_group, source_row):
     rows_here = panel.shape[0]
     columns = panel.shape[1]
     groups = lax.axis_size("grp")
@@ -160,12 +384,23 @@
     panel_total = rows_here * devices * groups
     sketch = gathered * (1.0 / math.sqrt(panel_total))
     sketch_total = sketch.shape[0] * devices * groups
-    if sketch_total <= rows_here:
-        pieces = lax.all_gather(sketch, ("grp", "dev"), axis=0, tiled=True)
+    partial_gram = jnp.dot(sketch.T, sketch, precision=highest, preferred_element_type=jnp.float32)
+    return sketch, lax.psum(partial_gram, ("grp", "dev"))
+
+
+def on_device(panel, signs, source_group, source_row):
+    rows_here, columns = panel.shape
+    groups = lax.axis_size("grp")
+    devices = lax.axis_size("dev")
+    highest = lax.Precision.HIGHEST
+    width = source_row.shape[2]
+    sketch_total = groups * devices * width
+    fits = groups & (groups - 1) == 0 and groups * width == 128 and rows_here % 128 == 0
+    if devices == 8 and fits and rows_here & (rows_here - 1) == 0:
+        pieces, sketch = kernel_sketch(panel, signs, source_group, source_row, groups, devices)
         kernel = functools.partial(gram_kernel, sketch_total)
     else:
-        partial_gram = jnp.dot(sketch.T, sketch, precision=highest, preferred_element_type=jnp.float32)
-        pieces = lax.psum(partial_gram, ("grp", "dev"))
+        sketch, pieces = general_sketch(panel, signs, source_group, source_row)
         kernel = functools.partial(from_gram_kernel, sketch_total)
     inverse = pl.pallas_call(
         kernel,

time: 188 us -> 95 us (0.51)
  waiting for transfers between devices: 102 us -> 0 us
  Pallas kernels: 27.9 us -> 78.6 us
  matrix products: 23.1 us -> 6.14 us
  between operations: 14.1 us -> 0.66 us
  starting transfers between devices: 9.66 us -> 0 us
  other arithmetic: 5.7 us -> 3.35 us
    all_gather x1 -> x0, waiting for transfers between devices: 56.4 us -> none  [on_device(): pieces = lax.all_gather(sketch, ('grp', 'dev'), axis=0, tiled=True)]
    pallas_call x0 -> x1, Pallas kernels: none -> 50.3 us  [kernel_sketch(): pl.pallas_call(functools.partial(sketch_kernel, groups, per_owner, scale)...]
    all_to_all x2 -> x0, waiting for transfers between devices: 25.9 us -> none  [the longest x1 25.9 us: on_device(): lax.all_to_all(local.reshape(devices, rows_here // devices, columns), 'de...]
    reduce_scatter x1 -> x0, waiting for transfers between devices: 19.5 us -> none  [on_device(): lax.psum_scatter(inner[flat_index] * factor[:, None], 'grp', scatter_dime...]
    dot_general x2 -> x0, matrix products: 17.6 us -> none  [the longest x1 14.7 us: on_device(): jnp.dot(sylvester(rows_here), flipped, precision=highest, preferred_eleme...]
    all_to_all x2 -> x0, starting transfers between devices: 9.4 us -> none  [the longest x1 5.2 us: on_device(): lax.all_to_all(stacked, 'dev', split_axis=2, concat_axis=2, tiled=True)]
    mul x2 -> x0, other arithmetic: 2.26 us -> none  [the longest x1 1.47 us: on_device(): sketch = gathered * (1.0 / math.sqrt(panel_total))]
    unnamed x3 -> x7, local copies, waits for them, and re-layouts: 2.43 us -> 4.06 us
  transfers between devices with their start and end apart: 4 -> 0, of which waited for: 3 -> 0; matrix products, arithmetic and copies ran while one was open for 8% -> 0% of each run, Pallas kernels for 0% -> 0%
where the time goes in v1:
time: 95 us; the launch traced here: 94.7 us
  Pallas kernels  78.6 us (83%)
  matrix products  6.14 us (6%)
  local copies, waits for them, and re-layouts  6.02 us (6%)
  other arithmetic  3.35 us (4%)
    pallas_call x1, Pallas kernels, kernel_sketch(): pl.pallas_call(functools.partial(sketch_kernel, groups, per_owner, scale)...  50.3 us
    pallas_call x1, Pallas kernels, on_device(): pl.pallas_call(kernel, out_shape=jax.ShapeDtypeStruct((columns, columns),...  28.3 us
    dot_general x1, matrix products, on_device(): lax.dot_general(panel, inverse, (((1,), (1,)), ((), ())), precision=highe...  6.14 us
    unnamed x7, local copies, waits for them, and re-layouts  4.06 us
    unnamed x2, other arithmetic  2.69 us

profile of v1, /device:TPU:0, one launch (start us, length us, event | category | flops | bytes accessed | tf_op | source)
XLA Modules:
  0.0 94.7 jit_solution(11064544538171592727)
XLA Ops:
  0.6 0.1 pad.2.clone
  0.7 0.5 broadcast.8
  1.2 1.3 %reduce.7 = s32[4,32]{1,0:T(4,128)S(1)} reduce(s32[4,1,32,1]{2,3,1,0:T(1,128)} %param.6, s32[]{:T(128)} %broadcast.8), dimensions={1,3}, to_apply=%param.6.reduce_sub_computation.3 | reduce | bytes 1028 | tf_op args[2]
  2.6 0.1 stack_reshape.6
  2.7 1.3 %reduce.6 = s32[4,32]{1,0:T(4,128)S(1)} reduce(s32[4,1,32]{2,1,0:T(1,128)} %param.7, s32[]{:T(128)} %broadcast.8), dimensions={1}, to_apply=%param.7.reduce_sub_computation.3 | reduce | bytes 1028 | tf_op args[3]
  4.0 0.1 stack_reshape.7
  4.1 0.7 add_add_fusion.picks_ref
  4.8 1.7 %copy.7.signs_ref = s32[1024,1]{1,0:T(8,128)} copy(s32[1024,1]{0,1:T(1,128)} %bitcast.8) | data formatting | bytes 8192 | tf_op jit(solution)/shard_map/broadcast_in_dim | solution.py:323
  6.5 50.3 %sketch.1 = (f32[8,128,512]{2,1,0:T(8,128)}, f32[32,512]{1,0:T(8,128)}) custom-call(f32[1024,512]{1,0:T(8,128)} %panel_ref.1, s32[1024,1]{1,0:T(8,128)} %copy.7.signs_ref, s32[8,128]{1,0:T(8,128)} %add_add_fusion.picks_ref), custom_call_target="tpu_custom_call" | custom-call | tf_op jit(solution)/shard_map/sketch/pallas_call | solution.py:300
  56.7 0.0 copy-start
  56.8 28.3 %factor.1 = f32[512,512]{1,0:T(8,128)} custom-call(f32[1024,512]{1,0:T(8,128)} %bitcast.7), custom_call_target="tpu_custom_call" | custom-call | tf_op jit(solution)/shard_map/factor/pallas_call | solution.py:405
  85.0 0.0 copy-done
  85.0 6.1 %convolution_bitcast_fusion = f32[1024,512]{0,1:T(8,128)} fusion(f32[512,512]{1,0:T(8,128)} %factor.1, f32[1024,512]{1,0:T(8,128)S(1)} %copy-done), kind=kOutput, calls=%fused_computation | convolution fusion | flops 3221225472 | bytes 5242880 | tf_op jit(solution)/shard_map/dot_general | solution.py:413
  91.2 0.0 copy-start.1
  91.2 2.9 %copy.8 = f32[1024,512]{1,0:T(8,128)} copy(f32[1024,512]{0,1:T(8,128)} %convolution_bitcast_fusion) | data formatting | bytes 4194304
  94.1 0.0 copy-done.1
  94.1 0.6 copy.10
  (1 shorter events, 0.0 us)
Async XLA Ops:
  56.7 28.3 %copy-start = (f32[1024,512]{1,0:T(8,128)S(1)}, f32[1024,512]{1,0:T(8,128)}, u32[]{:S(2)}) copy-start(f32[1024,512]{1,0:T(8,128)} %panel_ref.1) | copy-start | bytes 6291460
  91.2 2.9 %copy-start.1 = (f32[32,512]{1,0:T(8,128)S(1)}, f32[32,512]{1,0:T(8,128)}, u32[]{:S(2)}) copy-start(f32[32,512]{1,0:T(8,128)} %get-tuple-element.12) | copy-start | bytes 196612

commit v2 on v1

--- a/solution.py
+++ b/solution.py
@@ -87,17 +87,41 @@
     return gram / sketch_total + jnp.where(rowi == coli, 0.001, 0.0)
 
 
-def gram_kernel(sketch_total, sketch_ref, out_ref, work):
-    sketch = sketch_ref[...]
-    work[...] = add_ridge(matmul(sketch, sketch, ((0,), (0,))), sketch_total)
+def halves(value):
+    high = value.astype(jnp.bfloat16)
+    return high, (value - high.astype(jnp.float32)).astype(jnp.bfloat16)
+
+
+def split_matmul(a, b, dims):
+    dot = functools.partial(
+        lax.dot_general, dimension_numbers=(dims, ((), ())), preferred_element_type=jnp.float32
+    )
+    return dot(a[0], b[0]) + (dot(a[0], b[1]) + dot(a[1], b[0]))
+
+
+def finish(work, panel_ref, out_ref):
+    rows, columns = panel_ref.shape
+    part = columns // 2
+    for base in (0, part):
+        deep = base + part
+        factor = halves(work[base : base + part, 0:deep])
+        out_ref[:, base : base + part] = split_matmul(
+            halves(panel_ref[:, 0:deep]), factor, ((1,), (1,))
+        )
+
+
+def gram_kernel(sketch_total, sketch_ref, panel_ref, own_ref, out_ref, work):
+    own_ref[...] = sketch_ref[0 : own_ref.shape[0], :]
+    sketch = halves(sketch_ref[...])
+    work[...] = add_ridge(split_matmul(sketch, sketch, ((0,), (0,))), sketch_total)
     inverse_factor(work)
-    out_ref[...] = work[...]
-
-
-def from_gram_kernel(sketch_total, gram_ref, out_ref, work):
+    finish(work, panel_ref, out_ref)
+
+
+def from_gram_kernel(sketch_total, gram_ref, panel_ref, out_ref, work):
     work[...] = add_ridge(gram_ref[...], sketch_total)
     inverse_factor(work)
-    out_ref[...] = work[...]
+    finish(work, panel_ref, out_ref)
 
 
 def flip(index, mask):
@@ -120,8 +144,8 @@
 
 
 def sketch_kernel(
-    groups, per_owner, scale, panel_ref, signs_ref, picks_ref, whole_ref, own_ref,
-    lists, high, low, choice, acc, from_core, from_first, from_second, from_group, send, recv,
+    groups, per_owner, scale, panel_ref, signs_ref, group_ref, row_ref, whole_ref,
+    lists, values, high, low, choice, acc, from_core, from_first, from_second, from_group, send, recv,
 ):
     devices = 8
     rows_here, columns = panel_ref.shape
@@ -161,36 +185,36 @@
         return copy
 
     sends = []
-    listed = [transfer(picks_ref, lists.at[mask], "dev", mask) for mask in range(1, devices)]
-    flipped = panel_ref[...] * (1 - 2 * signs_ref[...]).astype(jnp.float32)
-    top = flipped.astype(jnp.bfloat16)
+    listed = [transfer(group_ref, lists.at[0, mask], "dev", mask) for mask in range(1, devices)]
+    listed += [transfer(row_ref, lists.at[1, mask], "dev", mask) for mask in range(1, devices)]
+    top = panel_ref[...].astype(jnp.bfloat16)
     high[...] = top
-    low[...] = (flipped - top.astype(jnp.float32)).astype(jnp.bfloat16)
-    lists[0] = picks_ref[...]
+    low[...] = (panel_ref[...] - top.astype(jnp.float32)).astype(jnp.bfloat16)
+    lists[0, 0] = group_ref[...]
+    lists[1, 0] = row_ref[...]
     for copy in listed:
         copy.wait_recv()
     sends += listed
 
-    slot = lax.broadcasted_iota(jnp.int32, (devices, band), 0)
-    group_of = jnp.concatenate([lists[m][0:1, :] for m in range(devices)], axis=0)
-    row_of = jnp.concatenate([lists[m][1:2, :] for m in range(devices)], axis=0)
-    value = (group_of * devices + (slot ^ me)) * rows_here + row_of
+    for slot in range(devices):
+        values[slot * groups : (slot + 1) * groups, :] = (
+            lists[0, slot] * devices + flip(me, slot)
+        ) * rows_here + lists[1, slot]
     total = devices * band
-    place = lax.broadcasted_iota(jnp.int32, (total, band), 0)
-    entry = lax.broadcasted_iota(jnp.int32, (total, band), 1)
-    owner = (place // band) ^ me
-    group = ((place // share) % groups) ^ here
-    wanted = group * share + owner * per_owner + place % per_owner
+    width = devices * per_owner
+    place = lax.broadcasted_iota(jnp.int32, (total, width), 0)
+    entry = lax.broadcasted_iota(jnp.int32, (total, width), 1)
+    wanted = ((place // band) ^ me) * per_owner + place % per_owner
     spread = lax.dot_general(
         (entry == wanted).astype(jnp.float32),
-        value.astype(jnp.float32),
+        values[...].astype(jnp.float32),
         (((1,), (1,)), ((), ())),
         precision=lax.Precision.HIGHEST,
         preferred_element_type=jnp.float32,
     )
-    place = lax.broadcasted_iota(jnp.int32, (total, devices), 0)
-    held = lax.broadcasted_iota(jnp.int32, (total, devices), 1)
-    source = ((place // per_owner) % devices) ^ me
+    place = lax.broadcasted_iota(jnp.int32, (total, devices * groups), 0)
+    held = lax.broadcasted_iota(jnp.int32, (total, devices * groups), 1)
+    source = (((place // per_owner) % devices) ^ me) * groups + (((place // share) % groups) ^ here)
     choice[...] = jnp.sum(jnp.where(held == source, spread, 0.0), axis=1, keepdims=True).astype(jnp.int32)
 
     def mixed(chunk):
@@ -204,6 +228,8 @@
             turn = (1 - 2 * ((pick >> bit) & 1)).astype(jnp.float32)
             table = table + [part * turn for part in table]
             bit = bit + 1
+        turns = (1 - 2 * signs_ref[...]).astype(jnp.float32)
+        table = [part * turns[i : i + 1, :] for i, part in enumerate(table)]
         table = jnp.concatenate([part.astype(jnp.bfloat16) for part in table], axis=1)
         dims = (((1,), (0,)), ((), ()))
         return lax.dot_general(
@@ -250,7 +276,6 @@
         result = result + from_group[block]
     sends += across
     result = result * scale
-    own_ref[...] = result
     whole_ref[0, 0:share, :] = result
 
     across = [
@@ -292,21 +317,17 @@
     per_owner = source_row.shape[2] // devices
     band = groups * devices * per_owner
     share = devices * per_owner
-    picks = jnp.stack([source_group.reshape(band), source_row.reshape(band)])
-    picks = jnp.concatenate([picks, jnp.zeros((6, band), jnp.int32)], axis=0)
     scale = 1.0 / math.sqrt(rows_here * devices * groups)
     vmem = pl.BlockSpec(memory_space=pltpu.VMEM)
     f32 = jnp.float32
-    whole, own = pl.pallas_call(
+    whole = pl.pallas_call(
         functools.partial(sketch_kernel, groups, per_owner, scale),
-        out_shape=(
-            jax.ShapeDtypeStruct((devices, band, columns), f32),
-            jax.ShapeDtypeStruct((share, columns), f32),
-        ),
-        in_specs=[vmem] * 3,
-        out_specs=(vmem, vmem),
+        out_shape=jax.ShapeDtypeStruct((devices, band, columns), f32),
+        in_specs=[vmem] * 4,
+        out_specs=vmem,
         scratch_shapes=[
-            pltpu.VMEM((devices, 8, band), jnp.int32),
+            pltpu.VMEM((2, devices, groups, share), jnp.int32),
+            pltpu.VMEM((devices * groups, share), jnp.int32),
             pltpu.VMEM((rows_here, columns), jnp.bfloat16),
             pltpu.VMEM((rows_here, columns), jnp.bfloat16),
             pltpu.VMEM((devices * band, 1), jnp.int32),
@@ -315,13 +336,18 @@
             pltpu.VMEM((2, band, columns), f32),
             pltpu.VMEM((band, columns), f32),
             pltpu.VMEM((groups, share, columns), f32),
-            pltpu.SemaphoreType.DMA((40,)),
-            pltpu.SemaphoreType.DMA((40,)),
+            pltpu.SemaphoreType.DMA((56,)),
+            pltpu.SemaphoreType.DMA((56,)),
         ],
         compiler_params=pltpu.CompilerParams(collective_id=0, has_side_effects=True),
         name="sketch",
-    )(panel, signs[:, None], picks)
-    return whole.reshape(devices * band, columns), own
+    )(
+        panel,
+        signs.reshape(rows_here // 128, 128),
+        source_group.reshape(groups, share),
+        source_row.reshape(groups, share),
+    )
+    return whole.reshape(devices * band, columns)
 
 
 def bit_parity(value, bits):
@@ -392,27 +418,25 @@
     rows_here, columns = panel.shape
     groups = lax.axis_size("grp")
     devices = lax.axis_size("dev")
-    highest = lax.Precision.HIGHEST
     width = source_row.shape[2]
     sketch_total = groups * devices * width
     fits = groups & (groups - 1) == 0 and groups * width == 128 and rows_here % 128 == 0
     if devices == 8 and fits and rows_here & (rows_here - 1) == 0:
-        pieces, sketch = kernel_sketch(panel, signs, source_group, source_row, groups, devices)
-        kernel = functools.partial(gram_kernel, sketch_total)
+        pieces = kernel_sketch(panel, signs, source_group, source_row, groups, devices)
+        kernel, shapes = gram_kernel, [(width, columns), (rows_here, columns)]
     else:
         sketch, pieces = general_sketch(panel, signs, source_group, source_row)
-        kernel = functools.partial(from_gram_kernel, sketch_total)
-    inverse = pl.pallas_call(
-        kernel,
-        out_shape=jax.ShapeDtypeStruct((columns, columns), jnp.float32),
-        in_specs=[pl.BlockSpec(memory_space=pltpu.VMEM)],
-        out_specs=pl.BlockSpec(memory_space=pltpu.VMEM),
+        kernel, shapes = from_gram_kernel, [(rows_here, columns)]
+    *own, conditioned = pl.pallas_call(
+        functools.partial(kernel, sketch_total),
+        out_shape=[jax.ShapeDtypeStruct(shape, jnp.float32) for shape in shapes],
+        in_specs=[pl.BlockSpec(memory_space=pltpu.VMEM)] * 2,
+        out_specs=[pl.BlockSpec(memory_space=pltpu.VMEM)] * len(shapes),
         scratch_shapes=[pltpu.VMEM((columns, columns), jnp.float32)],
         name="factor",
-    )(pieces)
-    conditioned = lax.dot_general(
-        panel, inverse, (((1,), (1,)), ((), ())), precision=highest, preferred_element_type=jnp.float32
-    )
+    )(pieces, panel)
+    if own:
+        sketch = own[0]
     return (sketch, conditioned)
 
 

time: 95 us -> 80 us (0.84)
  matrix products: 6.14 us -> 0 us
  local copies, waits for them, and re-layouts: 6.02 us -> 0 us
  other arithmetic: 3.35 us -> 0 us
    dot_general x1 -> x0, matrix products: 6.14 us -> none  [on_device(): lax.dot_general(panel, inverse, (((1,), (1,)), ((), ())), precision=highe...]
    unnamed x7 -> x0, local copies, waits for them, and re-layouts: 4.06 us -> none
    unnamed x2 -> x0, other arithmetic: 2.69 us -> none
    broadcast_in_dim x2 -> x0, local copies, waits for them, and re-layouts: 1.71 us -> none  [the longest x1 1.71 us: kernel_sketch(): signs[:, None]]
where the time goes in v2:
time: 80 us; the launch traced here: 79.9 us
  Pallas kernels  79.2 us (99%)
    pallas_call x1, Pallas kernels, kernel_sketch(): pl.pallas_call(functools.partial(sketch_kernel, groups, per_owner, scale)...  50.5 us
    pallas_call x1, Pallas kernels, on_device(): pl.pallas_call(functools.partial(kernel, sketch_total), out_shape=[jax.Sh...  28.8 us

profile of v2, /device:TPU:0, one launch (start us, length us, event | category | flops | bytes accessed | tf_op | source)
XLA Modules:
  0.0 79.9 jit_solution(17378747242533012268)
XLA Ops:
  0.6 50.5 %sketch.1 = f32[8,128,512]{2,1,0:T(8,128)} custom-call(f32[1024,512]{1,0:T(8,128)} %panel_ref.3, s32[8,128]{1,0:T(8,128)} %bitcast.5, s32[4,32]{1,0:T(4,128)} %bitcast.6, s32[4,32]{1,0:T(4,128)} %bitcast.7), custom_call_target="tpu_custom_call" | custom-call | tf_op jit(solution)/shard_map/sketch/pallas_call | solution.py:323
  51.1 28.8 %factor.1 = (f32[32,512]{1,0:T(8,128)}, f32[1024,512]{1,0:T(8,128)}) custom-call(f32[1024,512]{1,0:T(8,128)} %bitcast.4, f32[1024,512]{1,0:T(8,128)} %panel_ref.3), custom_call_target="tpu_custom_call" | custom-call | tf_op jit(solution)/shard_map/factor/pallas_call | solution.py:430

commit v3 on v2

--- a/solution.py
+++ b/solution.py
@@ -149,8 +149,9 @@
 ):
     devices = 8
     rows_here, columns = panel_ref.shape
-    half = columns // 2
-    left, right = pl.ds(0, half), pl.ds(half, half)
+    part = columns // 4
+    lefts, rights = (pl.ds(0, part), pl.ds(2 * part, part)), (pl.ds(part, part), pl.ds(3 * part, part))
+    both = (pl.ds(0, 2 * part), pl.ds(2 * part, 2 * part))
     band = groups * devices * per_owner
     share = devices * per_owner
     me = lax.axis_index("dev")
@@ -241,73 +242,110 @@
         acc[chunk] = mixed(chunk)
         core[chunk - 1] = transfer(acc.at[chunk], from_core.at[chunk // 2], "dev", 1)
     first, second = {}, {}
+
+    def send_first(chunk, turn):
+        left, right = lefts[turn], rights[turn]
+        if chunk & 2:
+            first[turn, "left", chunk - 2] = transfer(
+                acc.at[chunk, :, left], from_first.at[chunk // 4, :, left], "dev", 2
+            )
+        if chunk & 4:
+            first[turn, "right", chunk - 4] = transfer(
+                acc.at[chunk, :, right], from_first.at[(chunk & 2) // 2, :, right], "dev", 4
+            )
+
     for chunk in (6, 2, 4, 0):
         acc[chunk] = mixed(chunk)
         core[chunk].wait_recv()
         acc[chunk] = acc[chunk] + from_core[chunk // 2]
-        if chunk & 2:
-            first["left", chunk - 2] = transfer(
-                acc.at[chunk, :, left], from_first.at[chunk // 4, :, left], "dev", 2
+        send_first(chunk, 0)
+        if chunk == 4:
+            for late in (6, 2, 4):
+                send_first(late, 1)
+    for turn in range(2):
+        left, right = lefts[turn], rights[turn]
+        first[turn, "left", 4].wait_recv()
+        acc[4, :, left] = acc[4, :, left] + from_first[1, :, left]
+        second[turn, "left"] = transfer(acc.at[4, :, left], from_second.at[:, left], "dev", 4)
+        first[turn, "right", 2].wait_recv()
+        acc[2, :, right] = acc[2, :, right] + from_first[1, :, right]
+        second[turn, "right"] = transfer(acc.at[2, :, right], from_second.at[:, right], "dev", 2)
+    summed = []
+    for turn in range(2):
+        first[turn, "left", 0].wait_recv()
+        first[turn, "right", 0].wait_recv()
+        second[turn, "left"].wait_recv()
+        second[turn, "right"].wait_recv()
+        columns_now = both[turn]
+        acc[0, :, columns_now] = (
+            acc[0, :, columns_now] + from_first[0, :, columns_now] + from_second[:, columns_now]
+        )
+        summed.append([
+            transfer(
+                acc.at[0, pl.ds(block * share, share), columns_now],
+                from_group.at[block, :, columns_now],
+                "grp",
+                block,
             )
-        if chunk & 4:
-            first["right", chunk - 4] = transfer(
-                acc.at[chunk, :, right], from_first.at[(chunk & 2) // 2, :, right], "dev", 4
+            for block in range(1, groups)
+        ])
+    sends += list(core.values()) + list(first.values()) + list(second.values())
+
+    spread_out = []
+    for turn in range(2):
+        columns_now = both[turn]
+        result = acc[0, 0:share, columns_now]
+        for block in range(1, groups):
+            summed[turn][block - 1].wait_recv()
+            result = result + from_group[block, :, columns_now]
+        whole_ref[0, 0:share, columns_now] = result * scale
+        spread_out.append([
+            transfer(
+                whole_ref.at[0, pl.ds(0, share), columns_now],
+                whole_ref.at[0, pl.ds(block * share, share), columns_now],
+                "grp",
+                block,
             )
-    first["left", 4].wait_recv()
-    acc[4, :, left] = acc[4, :, left] + from_first[1, :, left]
-    second["left"] = transfer(acc.at[4, :, left], from_second.at[:, left], "dev", 4)
-    first["right", 2].wait_recv()
-    acc[2, :, right] = acc[2, :, right] + from_first[1, :, right]
-    second["right"] = transfer(acc.at[2, :, right], from_second.at[:, right], "dev", 2)
-    first["left", 0].wait_recv()
-    first["right", 0].wait_recv()
-    acc[0] = acc[0] + from_first[0]
-    second["left"].wait_recv()
-    second["right"].wait_recv()
-    acc[0] = acc[0] + from_second[...]
-    sends += list(core.values()) + list(first.values()) + list(second.values())
-    across = [
-        transfer(acc.at[0, pl.ds(block * share, share)], from_group.at[block], "grp", block)
-        for block in range(1, groups)
-    ]
-    result = acc[0, 0:share, :]
-    for block in range(1, groups):
-        across[block - 1].wait_recv()
-        result = result + from_group[block]
-    sends += across
-    result = result * scale
-    whole_ref[0, 0:share, :] = result
-
-    across = [
-        transfer(
-            whole_ref.at[0, pl.ds(0, share)], whole_ref.at[0, pl.ds(block * share, share)], "grp", block
-        )
-        for block in range(1, groups)
-    ]
-    for copy in across:
-        copy.wait_recv()
-    sends += across
-    out = [
-        transfer(whole_ref.at[0, :, left], whole_ref.at[4, :, left], "dev", 4),
-        transfer(whole_ref.at[0, :, right], whole_ref.at[2, :, right], "dev", 2),
-        transfer(whole_ref.at[0, :, left], whole_ref.at[2, :, left], "dev", 2),
-        transfer(whole_ref.at[0, :, right], whole_ref.at[4, :, right], "dev", 4),
-    ]
-    last = [transfer(whole_ref.at[0], whole_ref.at[1], "dev", 1)]
-    out[0].wait_recv()
-    relay = [transfer(whole_ref.at[4, :, left], whole_ref.at[6, :, left], "dev", 2)]
-    out[1].wait_recv()
-    relay.append(transfer(whole_ref.at[2, :, right], whole_ref.at[6, :, right], "dev", 4))
-    out[2].wait_recv()
-    last.append(transfer(whole_ref.at[2], whole_ref.at[3], "dev", 1))
-    out[3].wait_recv()
-    last.append(transfer(whole_ref.at[4], whole_ref.at[5], "dev", 1))
-    relay[0].wait_recv()
-    relay[1].wait_recv()
-    last.append(transfer(whole_ref.at[6], whole_ref.at[7], "dev", 1))
+            for block in range(1, groups)
+        ])
+        sends += summed[turn]
+    out, relay, last = [], [], []
+
+    def hand_over(chunk, turn):
+        columns_now = both[turn]
+        last.append(
+            transfer(whole_ref.at[chunk, :, columns_now], whole_ref.at[chunk + 1, :, columns_now], "dev", 1)
+        )
+
+    for turn in range(2):
+        left, right = lefts[turn], rights[turn]
+        for copy in spread_out[turn]:
+            copy.wait_recv()
+        out.append([
+            transfer(whole_ref.at[0, :, left], whole_ref.at[4, :, left], "dev", 4),
+            transfer(whole_ref.at[0, :, right], whole_ref.at[2, :, right], "dev", 2),
+            transfer(whole_ref.at[0, :, left], whole_ref.at[2, :, left], "dev", 2),
+            transfer(whole_ref.at[0, :, right], whole_ref.at[4, :, right], "dev", 4),
+        ])
+        hand_over(0, turn)
+        sends += spread_out[turn] + out[turn]
+    for turn in range(2):
+        left, right = lefts[turn], rights[turn]
+        out[turn][0].wait_recv()
+        relay.append(transfer(whole_ref.at[4, :, left], whole_ref.at[6, :, left], "dev", 2))
+        out[turn][1].wait_recv()
+        relay.append(transfer(whole_ref.at[2, :, right], whole_ref.at[6, :, right], "dev", 4))
+        out[turn][2].wait_recv()
+        hand_over(2, turn)
+        out[turn][3].wait_recv()
+        hand_over(4, turn)
+    for turn in range(2):
+        relay[2 * turn].wait_recv()
+        relay[2 * turn + 1].wait_recv()
+        hand_over(6, turn)
     for copy in last:
         copy.wait_recv()
-    sends += out + relay + last
+    sends += relay + last
     for copy in sends:
         copy.wait_send()
 
@@ -336,8 +374,8 @@
             pltpu.VMEM((2, band, columns), f32),
             pltpu.VMEM((band, columns), f32),
             pltpu.VMEM((groups, share, columns), f32),
-            pltpu.SemaphoreType.DMA((56,)),
-            pltpu.SemaphoreType.DMA((56,)),
+            pltpu.SemaphoreType.DMA((72,)),
+            pltpu.SemaphoreType.DMA((72,)),
         ],
         compiler_params=pltpu.CompilerParams(collective_id=0, has_side_effects=True),
         name="sketch",
@@ -420,7 +458,7 @@
     devices = lax.axis_size("dev")
     width = source_row.shape[2]
     sketch_total = groups * devices * width
-    fits = groups & (groups - 1) == 0 and groups * width == 128 and rows_here % 128 == 0
+    fits = groups & (groups - 1) == 0 and groups * width == 128 and columns % 512 == 0 and rows_here % 128 == 0
     if devices == 8 and fits and rows_here & (rows_here - 1) == 0:
         pieces = kernel_sketch(panel, signs, source_group, source_row, groups, devices)
         kernel, shapes = gram_kernel, [(width, columns), (rows_here, columns)]

time: 80 us -> 78.7 us (0.984)
  Pallas kernels: 79.2 us -> 77.9 us
    pallas_call x1, Pallas kernels: 50.5 us -> 49.2 us  [kernel_sketch(): pl.pallas_call(functools.partial(sketch_kernel, groups, per_owner, scale)...]
where the time goes in v3:
time: 78.7 us; the launch traced here: 78.6 us
  Pallas kernels  77.9 us (99%)
    pallas_call x1, Pallas kernels, kernel_sketch(): pl.pallas_call(functools.partial(sketch_kernel, groups, per_owner, scale)...  49.2 us
    pallas_call x1, Pallas kernels, on_device(): pl.pallas_call(functools.partial(kernel, sketch_total), out_shape=[jax.Sh...  28.8 us

profile of v3, /device:TPU:0, one launch (start us, length us, event | category | flops | bytes accessed | tf_op | source)
XLA Modules:
  0.0 78.6 jit_solution(2510645682853936263)
XLA Ops:
  0.6 49.2 %sketch.1 = f32[8,128,512]{2,1,0:T(8,128)} custom-call(f32[1024,512]{1,0:T(8,128)} %panel_ref.3, s32[8,128]{1,0:T(8,128)} %bitcast.5, s32[4,32]{1,0:T(4,128)} %bitcast.6, s32[4,32]{1,0:T(4,128)} %bitcast.7), custom_call_target="tpu_custom_call" | custom-call | tf_op jit(solution)/shard_map/sketch/pallas_call | solution.py:361
  49.8 28.8 %factor.1 = (f32[32,512]{1,0:T(8,128)}, f32[1024,512]{1,0:T(8,128)}) custom-call(f32[1024,512]{1,0:T(8,128)} %bitcast.4, f32[1024,512]{1,0:T(8,128)} %panel_ref.3), custom_call_target="tpu_custom_call" | custom-call | tf_op jit(solution)/shard_map/factor/pallas_call | solution.py:468

commit v4 on v3

--- a/solution.py
+++ b/solution.py
@@ -45,12 +45,6 @@
     return tiles
 
 
-def matmul(a, b, dims):
-    return lax.dot_general(
-        a, b, (dims, ((), ())), precision=lax.Precision.HIGHEST, preferred_element_type=jnp.float32
-    )
-
-
 def inverse_factor(work):
     size = work.shape[0]
     rowi = lax.broadcasted_iota(jnp.int32, (BLOCK, BLOCK), 0)
@@ -65,15 +59,19 @@
         ]
         tiles = pivot_block(tiles)
         own = jnp.where(rowi >= coli, jnp.concatenate(tiles, axis=0), 0.0)
-        rows = matmul(own, work[here, :], ((1,), (0,)))
+        rows = split_matmul(halves(own), halves(work[here, :]), ((1,), (0,)))
         work[here, :] = rows
         work[here, here] = own
         rows = work[here, :]
-        work[:, here] = jnp.where(
-            lax.broadcasted_iota(jnp.int32, (size, BLOCK), 0) >= start + BLOCK, 0.0, work[:, here]
-        )
-        left = jnp.where(wide >= start + BLOCK, rows, 0.0)
-        work[...] = work[...] - matmul(left, rows, ((0,), (0,)))
+
+        @pl.when(start + BLOCK < size)
+        def _():
+            work[:, here] = jnp.where(
+                lax.broadcasted_iota(jnp.int32, (size, BLOCK), 0) >= start + BLOCK, 0.0, work[:, here]
+            )
+            left = jnp.where(wide >= start + BLOCK, rows, 0.0)
+            work[...] = work[...] - split_matmul(halves(left), halves(rows), ((0,), (0,)))
+
         work[here, :] = jnp.where(wide < start + BLOCK, rows, 0.0)
         return carry
 

time: 78.7 us -> 76.3 us (0.970)
  Pallas kernels: 77.9 us -> 75.5 us
    pallas_call x1, Pallas kernels: 28.8 us -> 26.3 us  [on_device(): pl.pallas_call(functools.partial(kernel, sketch_total), out_shape=[jax.Sh...]
where the time goes in v4:
time: 76.3 us; the launch traced here: 76.1 us
  Pallas kernels  75.5 us (99%)
    pallas_call x1, Pallas kernels, kernel_sketch(): pl.pallas_call(functools.partial(sketch_kernel, groups, per_owner, scale)...  49.2 us
    pallas_call x1, Pallas kernels, on_device(): pl.pallas_call(functools.partial(kernel, sketch_total), out_shape=[jax.Sh...  26.3 us

profile of v4, /device:TPU:0, one launch (start us, length us, event | category | flops | bytes accessed | tf_op | source)
XLA Modules:
  0.0 76.1 jit_solution(871234609910610187)
XLA Ops:
  0.6 49.2 %sketch.1 = f32[8,128,512]{2,1,0:T(8,128)} custom-call(f32[1024,512]{1,0:T(8,128)} %panel_ref.3, s32[8,128]{1,0:T(8,128)} %bitcast.5, s32[4,32]{1,0:T(4,128)} %bitcast.6, s32[4,32]{1,0:T(4,128)} %bitcast.7), custom_call_target="tpu_custom_call" | custom-call | tf_op jit(solution)/shard_map/sketch/pallas_call | solution.py:359
  49.8 26.3 %factor.1 = (f32[32,512]{1,0:T(8,128)}, f32[1024,512]{1,0:T(8,128)}) custom-call(f32[1024,512]{1,0:T(8,128)} %bitcast.4, f32[1024,512]{1,0:T(8,128)} %panel_ref.3), custom_call_target="tpu_custom_call" | custom-call | tf_op jit(solution)/shard_map/factor/pallas_call | solution.py:466
